TPU v7x, 256 devices: a whole 4x4x8 slice. The times are simulated.
256 devices in a mesh: tm: 64 (over y_hi, x, z), rows: 4 (over y_lo, core).
Axes of the slice: x: 4, y: 4 (y_hi: 2, y_lo: 2; y = y_hi * 2 + y_lo), z: 8, core: 2. Of those that a mesh axis runs over, the one named last changes fastest.
Arguments:
- frames: bfloat16 [64, 32, 32, 640], P('tm', 'rows'), may hold values from -24 to 24
- conv_weight: bfloat16 [3, 3, 640, 640], replicated, may hold values from -0.078125 to 0.078125
- conv_bias: float32 [640], replicated, may hold values from -1.5 to 1.5
- ref_features: bfloat16 [1024, 640], P('tm'), may hold values from -6 to 6
- w_query: bfloat16 [640, 640], replicated, may hold values from -0.25 to 0.25
- w_key: bfloat16 [640, 640], replicated, may hold values from -0.25 to 0.25
- w_value: bfloat16 [640, 640], replicated, may hold values from -0.25 to 0.25
- w_out: bfloat16 [640, 640], replicated, may hold values from -0.25 to 0.25
- out_bias: float32 [640], replicated, may hold values from -1.5 to 1.5
Outputs:
- hidden: bfloat16 [64, 32, 32, 640], P('tm', 'rows')
- attended: bfloat16 [64, 32, 32, 640], P('tm', 'rows')
All inputs are finite; a program needn't handle non-finite values.
Results may differ from a plain program's by a relative error of at most 0.025.
Values may be sent and summed in bfloat16 or wider, within the bound.
A program may use at most 128 MiB of HBM per device.

v0:
```python
import jax
import jax.numpy as jnp
from jax import lax
from jax.sharding import PartitionSpec as P

HD = 80
key_block = 1024


def extended(value, sides, width):
    for axis, dim in sides:
        size, length = (lax.axis_size(axis), value.shape[dim])
        up = [(i, (i + 1) % size) for i in range(size - 1)]
        down = [(j, i) for i, j in up]
        last = lax.slice_in_dim(value, length - width, length, axis=dim)
        initial = lax.slice_in_dim(value, 0, width, axis=dim)
        before = lax.ppermute(last, axis, up)
        after = lax.ppermute(initial, axis, down)
        value = jnp.concatenate([before, value, after], axis=dim)
    return value


def attend_update(carry, query_heads, keys, values, heads):
    top, total, summed = carry
    count, band = (query_heads.shape[0], query_heads.shape[1])
    length = keys.shape[1]
    summed = summed.reshape(count, band, heads, HD)
    width = min(key_block, length)
    key_part = keys.reshape(keys.shape[0], width, heads, HD)
    value_part = values.reshape(values.shape[0], width, heads, HD)
    scores = jnp.einsum(
        "fqhd,khd->fhqk", query_heads, key_part[0], preferred_element_type=jnp.float32
    )
    scores = scores * HD ** (-0.5)
    new_top = jnp.maximum(top, jnp.max(scores, axis=3))
    factor = jnp.exp(top - new_top)
    weights = jnp.exp(scores - new_top[..., None])
    total = total * factor + jnp.sum(weights, axis=3)
    product = jnp.einsum(
        "fhqk,khd->fqhd",
        weights.astype(jnp.bfloat16),
        value_part[0],
        preferred_element_type=jnp.float32,
    )
    summed = summed * jnp.transpose(factor, (0, 2, 1))[..., None] + product
    return (new_top, total, summed.reshape(count, band, heads * HD))


def project_pair(source, w_key, w_value, count, channels):
    key = (
        jnp.dot(source, w_key, preferred_element_type=jnp.float32)
        .astype(jnp.bfloat16)
        .reshape(count, -1, channels)
    )
    value = (
        jnp.dot(source, w_value, preferred_element_type=jnp.float32)
        .astype(jnp.bfloat16)
        .reshape(count, -1, channels)
    )
    return (key, value)


def shards(frames, conv_weight, conv_bias, ref_features, w_query, w_key, w_value, w_out, out_bias):
    count, band_rows, width, channels = frames.shape
    heads = channels // HD
    band = band_rows * width
    activated = jax.nn.silu(frames.astype(jnp.float32)).astype(jnp.bfloat16)
    padded = extended(activated, (("rows", 1),), 1)
    padded = jnp.pad(padded, ((0, 0), (0, 0), (1, 1), (0, 0)))
    convolved = jnp.zeros((count * band, channels), jnp.float32)
    for row_tap in range(3):
        for col_tap in range(3):
            window = padded[:, row_tap : row_tap + band_rows, col_tap : col_tap + width].reshape(
                count * band, channels
            )
            convolved = convolved + jnp.dot(
                window, conv_weight[row_tap, col_tap], preferred_element_type=jnp.float32
            )
    hidden = (
        frames.reshape(count * band, channels).astype(jnp.float32) + convolved + conv_bias
    ).astype(jnp.bfloat16)
    query = jnp.dot(hidden, w_query, preferred_element_type=jnp.float32).astype(jnp.bfloat16)
    query_heads = query.reshape(count, band, heads, HD)
    start_state = (
        jnp.full((count, heads, band), -1e30, jnp.float32),
        jnp.zeros((count, heads, band), jnp.float32),
        jnp.zeros((count, band, channels), jnp.float32),
    )
    key, value = project_pair(hidden, w_key, w_value, count, channels)
    all_keys, all_values = (
        lax.all_gather(key, "rows", axis=1, tiled=True),
        lax.all_gather(value, "rows", axis=1, tiled=True),
    )
    state = attend_update(start_state, query_heads, all_keys, all_values, heads)
    ref_key = jnp.dot(ref_features, w_key, preferred_element_type=jnp.float32).astype(jnp.bfloat16)
    ref_value = jnp.dot(ref_features, w_value, preferred_element_type=jnp.float32).astype(
        jnp.bfloat16
    )
    every_key, every_value = (
        lax.all_gather(ref_key, "tm", axis=0, tiled=True),
        lax.all_gather(ref_value, "tm", axis=0, tiled=True),
    )
    state = attend_update(state, query_heads, every_key[None], every_value[None], heads)
    top, total, summed = state
    mixed = summed.reshape(count, band, heads, HD) / jnp.transpose(total, (0, 2, 1))[..., None]
    mixed = mixed.reshape(count * band, channels).astype(jnp.bfloat16)
    attended = (jnp.dot(mixed, w_out, preferred_element_type=jnp.float32) + out_bias).astype(
        jnp.bfloat16
    )
    return (
        hidden.reshape(count, band_rows, width, channels),
        attended.reshape(count, band_rows, width, channels),
    )


def solution(mesh):
    return jax.shard_map(
        shards,
        mesh=mesh,
        in_specs=(P("tm", "rows", None, None), P(), P(), P("tm", None), P(), P(), P(), P(), P()),
        out_specs=(P("tm", "rows", None, None), P("tm", "rows", None, None)),
        check_vma=False,
    )
```

profile of v0, /device:TPU:2, one launch (start us, length us, event | category | flops | bytes accessed | tf_op | source)
XLA Modules:
  0.0 329.9 jit_solution(8142130882859470929)
XLA Ops:
  7.2 1.3 multiply_convert_fusion
  8.6 2.0 collective-permute-start
  10.6 1.3 collective-permute-start.1
  11.9 3.2 collective-permute-done.1
  15.4 1.6 fusion.52
  21.0 1.2 convolution_convert_fusion.2
  22.2 1.2 convolution_convert_fusion
  23.5 0.8 convolution_convert_fusion.4
  24.6 0.8 convolution_convert_fusion.3
  26.1 26.4 %all-gather.11.cloned.1.call-done = bf16[1024,640]{1,0:T(8,128)(2,1)} async-done(((bf16[256,640]{1,0:T(8,128)(2,1)}), bf16[1024,640]{1,0:T(8,128)(2,1)}) %all-gather.11.cloned.1.call-update) | async-done | bytes 1310736 | tf_op jit(solution)/shard_map/all_gather | solution.py:91
  52.5 1.6 copy.19
  54.1 4.6 %bitcast_reduce_fusion.1 = (f32[8,256]{1,0:T(8,128)S(1)}, f32[8,1024,256]{2,1,0:T(8,128)}) fusion(bf16[1024,8,80]{0,2,1:T(8,128)(2,1)S(1)} %bitcast.200, bf16[256,8,80]{0,2,1:T(8,128)(2,1)S(1)} %bitcast.201), kind=kOutput, calls=%fused_computation.4 | convolution fusion | flops 339736576 | bytes 10035200 | tf_op jit(solution)/shard_map/fqhd,khd->fhqk/dot_general | solution.py:31
  58.7 22.4 %all-gather.13.cloned.1.call-done = bf16[1024,640]{1,0:T(8,128)(2,1)} async-done(((bf16[256,640]{1,0:T(8,128)(2,1)}), bf16[1024,640]{1,0:T(8,128)(2,1)}) %all-gather.13.cloned.1.call-update) | async-done | bytes 1310736 | tf_op jit(solution)/shard_map/all_gather | solution.py:92
  81.1 1.6 copy.21
  82.7 118.1 %all-gather.7.cloned.1.call-done = bf16[1024,640]{1,0:T(8,128)(2,1)} async-done(((bf16[16,640]{1,0:T(8,128)(2,1)}), bf16[1024,640]{1,0:T(8,128)(2,1)}) %all-gather.7.cloned.1.call-update) | async-done | bytes 1310736 | tf_op jit(solution)/shard_map/all_gather | solution.py:100
  200.9 1.6 copy.23
  202.5 2.4 bitcast_reduce_fusion
  204.9 1.1 copy-done.1
  206.0 2.7 fusion.2
  208.8 1.6 fusion.31
  210.4 105.2 %all-gather.9.cloned.1.call-done = bf16[1024,640]{1,0:T(8,128)(2,1)} async-done(((bf16[16,640]{1,0:T(8,128)(2,1)}), bf16[1024,640]{1,0:T(8,128)(2,1)}) %all-gather.9.cloned.1.call-update) | async-done | bytes 1310736 | tf_op jit(solution)/shard_map/all_gather | solution.py:101
  315.6 1.6 copy.24
  317.2 5.0 %fusion.40 = bf16[1,256,8,80]{1,3,2,0:T(8,128)(2,1)S(1)} fusion(f32[1,256,8,80]{1,3,2,0:T(8,128)S(1)} %fusion.31, bf16[1024,8,80]{0,2,1:T(8,128)(2,1)S(1)} %bitcast.206, f32[8,1024,256]{2,1,0:T(8,128)} %copy-done.2, f32[8,256]{1,0:T(8,128)S(1)} %get-tuple-element.15, f32[256,8]{0,1:T(8,128)S(1)} %get-tuple-element.12), kind=kOutput, calls=%fused_computation.45 | convolution fusion | flops 342327296 | bytes 10698752 | tf_op jit(solution)/shard_map/fhqk,khd->fqhd/dot_general | solution.py:39
  322.2 1.2 fusion.34
  (50 shorter events, 5.3 us)
Async XLA Ops:
  7.2 13.8 %copy-start = (bf16[640,640]{1,0:T(8,128)(2,1)S(1)}, bf16[640,640]{1,0:T(8,128)(2,1)}, u32[]{:S(2)}) copy-start(bf16[640,640]{1,0:T(8,128)(2,1)} %param.14) | copy-start | bytes 2457604
  7.2 45.3 %all-gather.11.cloned.1.call-start = ((), (), s32[]{:S(2)}) async-start(), calls=%async_computation.2 | async-start | bytes 1638400 | tf_op jit(solution)/shard_map/all_gather | solution.py:91
  7.2 9.8 %copy-start.3 = (bf16[3,3,640,640]{3,2,1,0:T(8,128)(2,1)S(1)}, bf16[3,3,640,640]{3,2,1,0:T(8,128)(2,1)}, u32[]{:S(2)}) copy-start(bf16[3,3,640,640]{3,2,1,0:T(8,128)(2,1)} %param.10) | copy-start | bytes 22118404
  8.6 3.3 %collective-permute-start = (bf16[1,1,32,640]{3,2,1,0:T(8,128)(2,1)S(1)}, bf16[1,1,32,640]{3,2,1,0:T(8,128)(2,1)S(1)}, u32[]{:S(2)}, u32[]{:S(2)}) collective-permute-start(bf16[1,1,32,640]{3,2,1,0:T(8,128)(2,1)S(1)} %get-tuple-element.10), channel_id=1, source_target_pairs={{0,1},{1,2},{2,3},{4,5},{5,6},{6,7},{8,9},{9,10},{10,11},{12,13},{... | collective-permute-start | bytes 122888 | tf_op jit(solution)/shard_map/ppermute | solution.py:17
  10.6 4.5 %collective-permute-start.1 = (bf16[1,1,32,640]{3,2,1,0:T(8,128)(2,1)S(1)}, bf16[1,1,32,640]{3,2,1,0:T(8,128)(2,1)S(1)}, u32[]{:S(2)}, u32[]{:S(2)}) collective-permute-start(bf16[1,1,32,640]{3,2,1,0:T(8,128)(2,1)S(1)} %get-tuple-element.11), channel_id=1, source_target_pairs={{1,0},{2,1},{3,2},{5,4},{6,5},{7,6},{9,8},{10,9},{11,10},{13,12},{... | collective-permute-start | bytes 122888 | tf_op jit(solution)/shard_map/ppermute | solution.py:18
  17.6 2.9 copy-start.7
  17.6 2.9 copy-start.10
  18.5 3.7 %copy-start.5 = (bf16[640,640]{1,0:T(8,128)(2,1)S(1)}, bf16[640,640]{1,0:T(8,128)(2,1)}, u32[]{:S(2)}) copy-start(bf16[640,640]{1,0:T(8,128)(2,1)} %param.15) | copy-start | bytes 2457604
  19.0 4.5 %copy-start.9 = (bf16[16,640]{1,0:T(8,128)(2,1)S(1)}, bf16[16,640]{1,0:T(8,128)(2,1)}, u32[]{:S(2)}) copy-start(bf16[16,640]{1,0:T(8,128)(2,1)} %param.12) | copy-start | bytes 61444
  19.0 6.4 %copy-start.8 = (bf16[640,640]{1,0:T(8,128)(2,1)S(1)}, bf16[640,640]{1,0:T(8,128)(2,1)}, u32[]{:S(2)}) copy-start(bf16[640,640]{1,0:T(8,128)(2,1)} %param.13) | copy-start | bytes 2457604
  21.0 37.7 %copy-start.4 = (bf16[256,640]{1,0:T(8,128)(2,1)}, bf16[256,640]{1,0:T(8,128)(2,1)S(1)}, u32[]{:S(2)}) copy-start(bf16[256,640]{1,0:T(8,128)(2,1)S(1)} %fusion.35) | copy-start | bytes 983044
  22.2 58.9 %all-gather.13.cloned.1.call-start = ((), (), s32[]{:S(2)}) async-start(), calls=%async_computation.3 | async-start | bytes 1638400 | tf_op jit(solution)/shard_map/all_gather | solution.py:92
  23.5 177.4 %all-gather.7.cloned.1.call-start = ((), (), s32[]{:S(2)}) async-start(), calls=%async_computation | async-start | bytes 1331200 | tf_op jit(solution)/shard_map/all_gather | solution.py:100
  24.4 291.2 %all-gather.9.cloned.1.call-start = ((), (), s32[]{:S(2)}) async-start(), calls=%async_computation.1 | async-start | bytes 1331200 | tf_op jit(solution)/shard_map/all_gather | solution.py:101
  26.1 56.6 %copy-start.6 = (bf16[256,640]{0,1:T(8,128)(2,1)}, bf16[256,640]{0,1:T(8,128)(2,1)S(1)}, u32[]{:S(2)}) copy-start(bf16[256,640]{0,1:T(8,128)(2,1)S(1)} %copy.20) | copy-start | bytes 983044
  202.5 3.6 %copy-start.1 = (f32[8,1024,256]{2,1,0:T(8,128)S(1)}, f32[8,1024,256]{2,1,0:T(8,128)}, u32[]{:S(2)}) copy-start(f32[8,1024,256]{2,1,0:T(8,128)} %get-tuple-element.20) | copy-start | bytes 25165828
  204.9 3.9 %copy-start.2 = (f32[8,1024,256]{2,1,0:T(8,128)}, f32[8,1024,256]{2,1,0:T(8,128)S(1)}, u32[]{:S(2)}) copy-start(f32[8,1024,256]{2,1,0:T(8,128)S(1)} %get-tuple-element.18) | copy-start | bytes 25165828
  210.4 111.8 %copy-start.12 = (f32[640]{0:T(1024)S(1)}, f32[640]{0:T(1024)}, u32[]{:S(2)}) copy-start(f32[640]{0:T(1024)} %param.17) | copy-start | bytes 7684
  317.2 5.0 %copy-start.11 = (bf16[640,640]{1,0:T(8,128)(2,1)S(1)}, bf16[640,640]{1,0:T(8,128)(2,1)}, u32[]{:S(2)}) copy-start(bf16[640,640]{1,0:T(8,128)(2,1)} %param.16) | copy-start | bytes 2457604
Sparse Core Ops, SparseCore 0:
  22.3 30.1 all-gather.10
  54.9 26.1 all-gather.12
  84.7 116.1 all-gather.6
  204.3 111.2 all-gather.8
where the time goes:
time: 330 us
  waiting for transfers between devices  275 us (83%)
  matrix products  24.5 us (7%)
  between operations  14.1 us (4%)
  local copies, waits for them, and re-layouts  7.96 us (2%)
  other arithmetic  4.31 us (1%)
  starting transfers between devices  3.64 us (1%)
    all_gather x1, waiting for transfers between devices, shards(): lax.all_gather(ref_key, 'tm', axis=0, tiled=True)  118 us
    all_gather x1, waiting for transfers between devices, shards(): lax.all_gather(ref_value, 'tm', axis=0, tiled=True)  105 us
    all_gather x1, waiting for transfers between devices, shards(): lax.all_gather(key, 'rows', axis=1, tiled=True)  26.4 us
    all_gather x1, waiting for transfers between devices, shards(): lax.all_gather(value, 'rows', axis=1, tiled=True)  22.4 us
    dot_general x2, matrix products, attend_update(): jnp.einsum('fqhd,khd->fhqk', query_heads, key_part[0], preferred_element_...  6.98 us
  transfers between devices with their start and end apart: 6, of which 5 were waited for; matrix products, arithmetic and copies ran while one was open for 6% of the time, Pallas kernels for 0%

commit v1 on v0

--- a/solution.py
+++ b/solution.py
@@ -88,7 +88,9 @@
     )
     key, value = project_pair(hidden, w_key, w_value, count, channels)
     all_keys, all_values = (
-        lax.all_gather(key, "rows", axis=1, tiled=True),
+        jnp.concatenate(
+            lax.all_to_all(jnp.stack([key] * lax.axis_size("rows")), "rows", 0, 0), axis=1
+        ),
         lax.all_gather(value, "rows", axis=1, tiled=True),
     )
     state = attend_update(start_state, query_heads, all_keys, all_values, heads)

time: 330 us -> 308 us (0.933)
  waiting for transfers between devices: 275 us -> 246 us
  starting transfers between devices: 3.64 us -> 7.35 us
    all_gather x1 -> x0, waiting for transfers between devices: 26.4 us -> none  [shards(): lax.all_gather(key, 'rows', axis=1, tiled=True)]
    all_gather x1, waiting for transfers between devices: 22.4 us -> 0.01 us  [shards(): lax.all_gather(value, 'rows', axis=1, tiled=True)]
    all_to_all x0 -> x1, waiting for transfers between devices: none -> 18.4 us  [shards(): lax.all_to_all(jnp.stack([key] * lax.axis_size('rows')), 'rows', 0, 0)]
    all_to_all x0 -> x1, starting transfers between devices: none -> 3.97 us  [shards(): lax.all_to_all(jnp.stack([key] * lax.axis_size('rows')), 'rows', 0, 0)]
  transfers between devices with their start and end apart: 6 -> 6, of which waited for: 5 -> 4; matrix products, arithmetic and copies ran while one was open for 6% -> 8% of each run, Pallas kernels for 0% -> 0%
where the time goes in v1:
time: 308 us
  waiting for transfers between devices  246 us (80%)
  matrix products  25.9 us (8%)
  between operations  14.1 us (5%)
  local copies, waits for them, and re-layouts  10.4 us (3%)
  starting transfers between devices  7.35 us (2%)
  other arithmetic  4.31 us (1%)
    all_gather x1, waiting for transfers between devices, shards(): lax.all_gather(ref_key, 'tm', axis=0, tiled=True)  119 us
    all_gather x1, waiting for transfers between devices, shards(): lax.all_gather(ref_value, 'tm', axis=0, tiled=True)  105 us
    all_to_all x1, waiting for transfers between devices, shards(): lax.all_to_all(jnp.stack([key] * lax.axis_size('rows')), 'rows', 0, 0)  18.4 us
    dot_general x2, matrix products, attend_update(): jnp.einsum('fqhd,khd->fhqk', query_heads, key_part[0], preferred_element_...  7.94 us
    dot_general x2, matrix products, attend_update(): jnp.einsum('fhqk,khd->fqhd', weights.astype(jnp.bfloat16), value_part[0],...  6.54 us
  transfers between devices with their start and end apart: 6, of which 4 were waited for; matrix products, arithmetic and copies ran while one was open for 8% of the time, Pallas kernels for 0%

profile of v1, /device:TPU:2, one launch (start us, length us, event | category | flops | bytes accessed | tf_op | source)
XLA Modules:
  0.0 307.6 jit_solution(5124590345611419357)
XLA Ops:
  7.2 1.3 multiply_convert_fusion
  8.6 2.0 collective-permute-start
  10.6 1.3 collective-permute-start.1
  11.9 3.2 %collective-permute-done.1 = bf16[1,1,32,640]{3,2,1,0:T(8,128)(2,1)S(1)} collective-permute-done((bf16[1,1,32,640]{3,2,1,0:T(8,128)(2,1)S(1)}, bf16[1,1,32,640]{3,2,1,0:T(8,128)(2,1)S(1)}, u32[]{:S(2)}, u32[]{:S(2)}) %collective-permute-start.1) | collective-permute-done | bytes 40992 | tf_op jit(solution)/shard_map/ppermute | solution.py:18
  15.4 1.6 fusion.52
  20.9 1.2 convolution_convert_fusion
  23.7 1.1 stack.3
  24.9 4.0 %all-to-all-start = ((bf16[4,1,256,640]{2,3,1,0:T(8,128)(2,1)}), bf16[4,1,256,640]{2,3,1,0:T(8,128)(2,1)S(1)}, u32[]{:S(2)}, u32[]{:S(2)}) async-start(bf16[4,1,256,640]{2,3,1,0:T(8,128)(2,1)} %stack.3), calls=%async_computation | async-start | bytes 2621440 | tf_op jit(solution)/shard_map/all_to_all | solution.py:92
  29.7 1.6 convolution_convert_fusion.1
  32.3 18.4 %all-to-all-done = bf16[4,1,256,640]{2,3,1,0:T(8,128)(2,1)S(1)} async-done(((bf16[4,1,256,640]{2,3,1,0:T(8,128)(2,1)}), bf16[4,1,256,640]{2,3,1,0:T(8,128)(2,1)S(1)}, u32[]{:S(2)}, u32[]{:S(2)}) %all-to-all-start) | async-done | bytes 1310752 | tf_op jit(solution)/shard_map/all_to_all | solution.py:92
  50.7 1.0 copy.27
  51.7 1.0 squeeze_reshape_reshape.3
  52.6 5.5 %bitcast_reduce_fusion.1 = (f32[8,256]{1,0:T(8,128)S(1)}, f32[8,1024,256]{2,1,0:T(8,128)}) fusion(bf16[1024,8,80]{0,2,1:T(8,128)(2,1)S(1)} %squeeze_reshape_reshape.3, bf16[256,8,80]{0,2,1:T(8,128)(2,1)} %bitcast.201), kind=kOutput, calls=%fused_computation.4 | convolution fusion | flops 339736576 | bytes 10035200 | tf_op jit(solution)/shard_map/fqhd,khd->fhqk/dot_general | solution.py:31
  58.2 1.6 copy.29
  59.8 118.6 %all-gather.5.cloned.1.call-done = bf16[1024,640]{1,0:T(8,128)(2,1)} async-done(((bf16[16,640]{1,0:T(8,128)(2,1)}), bf16[1024,640]{1,0:T(8,128)(2,1)}) %all-gather.5.cloned.1.call-update) | async-done | bytes 1310736 | tf_op jit(solution)/shard_map/all_gather | solution.py:102
  178.4 1.6 copy.31
  180.0 2.4 bitcast_reduce_fusion
  182.5 1.1 copy-done.1
  183.5 2.7 fusion.2
  186.3 1.6 fusion.31
  187.9 105.4 %all-gather.7.cloned.1.call-done = bf16[1024,640]{1,0:T(8,128)(2,1)} async-done(((bf16[16,640]{1,0:T(8,128)(2,1)}), bf16[1024,640]{1,0:T(8,128)(2,1)}) %all-gather.7.cloned.1.call-update) | async-done | bytes 1310736 | tf_op jit(solution)/shard_map/all_gather | solution.py:103
  293.3 1.6 copy.32
  294.9 5.0 %fusion.40 = bf16[1,256,8,80]{1,3,2,0:T(8,128)(2,1)S(1)} fusion(f32[1,256,8,80]{1,3,2,0:T(8,128)S(1)} %fusion.31, bf16[1024,8,80]{0,2,1:T(8,128)(2,1)S(1)} %bitcast.206, f32[8,1024,256]{2,1,0:T(8,128)} %copy-done.2, f32[8,256]{1,0:T(8,128)S(1)} %get-tuple-element.15, f32[256,8]{0,1:T(8,128)S(1)} %get-tuple-element.12), kind=kOutput, calls=%fused_computation.45 | convolution fusion | flops 342327296 | bytes 10698752 | tf_op jit(solution)/shard_map/fhqk,khd->fqhd/dot_general | solution.py:39
  299.9 1.2 fusion.34
  (48 shorter events, 7.6 us)
Async XLA Ops:
  7.2 15.0 %copy-start = (bf16[640,640]{1,0:T(8,128)(2,1)S(1)}, bf16[640,640]{1,0:T(8,128)(2,1)}, u32[]{:S(2)}) copy-start(bf16[640,640]{1,0:T(8,128)(2,1)} %param.14) | copy-start | bytes 2457604
  7.2 51.0 %all-gather.9.cloned.1.call-start = ((), (), s32[]{:S(2)}) async-start(), calls=%async_computation.3 | async-start | bytes 1638400 | tf_op jit(solution)/shard_map/all_gather | solution.py:94
  7.2 9.8 %copy-start.3 = (bf16[3,3,640,640]{3,2,1,0:T(8,128)(2,1)S(1)}, bf16[3,3,640,640]{3,2,1,0:T(8,128)(2,1)}, u32[]{:S(2)}) copy-start(bf16[3,3,640,640]{3,2,1,0:T(8,128)(2,1)} %param.10) | copy-start | bytes 22118404
  8.6 3.3 %collective-permute-start = (bf16[1,1,32,640]{3,2,1,0:T(8,128)(2,1)S(1)}, bf16[1,1,32,640]{3,2,1,0:T(8,128)(2,1)S(1)}, u32[]{:S(2)}, u32[]{:S(2)}) collective-permute-start(bf16[1,1,32,640]{3,2,1,0:T(8,128)(2,1)S(1)} %get-tuple-element.10), channel_id=1, source_target_pairs={{0,1},{1,2},{2,3},{4,5},{5,6},{6,7},{8,9},{9,10},{10,11},{12,13},{... | collective-permute-start | bytes 122888 | tf_op jit(solution)/shard_map/ppermute | solution.py:17
  10.6 4.5 %collective-permute-start.1 = (bf16[1,1,32,640]{3,2,1,0:T(8,128)(2,1)S(1)}, bf16[1,1,32,640]{3,2,1,0:T(8,128)(2,1)S(1)}, u32[]{:S(2)}, u32[]{:S(2)}) collective-permute-start(bf16[1,1,32,640]{3,2,1,0:T(8,128)(2,1)S(1)} %get-tuple-element.11), channel_id=1, source_target_pairs={{1,0},{2,1},{3,2},{5,4},{6,5},{7,6},{9,8},{10,9},{11,10},{13,12},{... | collective-permute-start | bytes 122888 | tf_op jit(solution)/shard_map/ppermute | solution.py:18
  17.6 2.8 copy-start.6
  17.6 2.8 copy-start.8
  18.1 2.8 copy-start.5
  18.5 3.7 %copy-start.7 = (bf16[16,640]{1,0:T(8,128)(2,1)S(1)}, bf16[16,640]{1,0:T(8,128)(2,1)}, u32[]{:S(2)}) copy-start(bf16[16,640]{1,0:T(8,128)(2,1)} %param.12) | copy-start | bytes 61444
  20.9 11.3 %copy-start.4 = (bf16[256,640]{1,0:T(8,128)(2,1)}, bf16[256,640]{1,0:T(8,128)(2,1)S(1)}, u32[]{:S(2)}) copy-start(bf16[256,640]{1,0:T(8,128)(2,1)S(1)} %fusion.35) | copy-start | bytes 983044
  22.1 156.2 %all-gather.5.cloned.1.call-start = ((), (), s32[]{:S(2)}) async-start(), calls=%async_computation.1 | async-start | bytes 1331200 | tf_op jit(solution)/shard_map/all_gather | solution.py:102
  24.9 25.8 %all-to-all-start = ((bf16[4,1,256,640]{2,3,1,0:T(8,128)(2,1)}), bf16[4,1,256,640]{2,3,1,0:T(8,128)(2,1)S(1)}, u32[]{:S(2)}, u32[]{:S(2)}) async-start(bf16[4,1,256,640]{2,3,1,0:T(8,128)(2,1)} %stack.3), calls=%async_computation | async-start | bytes 2621440 | tf_op jit(solution)/shard_map/all_to_all | solution.py:92
  28.9 264.4 %all-gather.7.cloned.1.call-start = ((), (), s32[]{:S(2)}) async-start(), calls=%async_computation.2 | async-start | bytes 1331200 | tf_op jit(solution)/shard_map/all_gather | solution.py:103
  180.0 3.6 %copy-start.1 = (f32[8,1024,256]{2,1,0:T(8,128)S(1)}, f32[8,1024,256]{2,1,0:T(8,128)}, u32[]{:S(2)}) copy-start(f32[8,1024,256]{2,1,0:T(8,128)} %get-tuple-element.20) | copy-start | bytes 25165828
  182.4 3.9 %copy-start.2 = (f32[8,1024,256]{2,1,0:T(8,128)}, f32[8,1024,256]{2,1,0:T(8,128)S(1)}, u32[]{:S(2)}) copy-start(f32[8,1024,256]{2,1,0:T(8,128)S(1)} %get-tuple-element.18) | copy-start | bytes 25165828
  187.9 112.0 %copy-start.10 = (f32[640]{0:T(1024)S(1)}, f32[640]{0:T(1024)}, u32[]{:S(2)}) copy-start(f32[640]{0:T(1024)} %param.17) | copy-start | bytes 7684
  294.9 5.0 %copy-start.9 = (bf16[640,640]{1,0:T(8,128)(2,1)S(1)}, bf16[640,640]{1,0:T(8,128)(2,1)}, u32[]{:S(2)}) copy-start(bf16[640,640]{1,0:T(8,128)(2,1)} %param.16) | copy-start | bytes 2457604
Sparse Core Ops, SparseCore 0:
  22.3 34.6 all-gather.8
  60.6 117.7 all-gather.4
  182.0 111.2 all-gather.6
